TPU v7x, 32 devices: a whole 2x2x4 slice. The times are simulated.
32 devices in a mesh: gx: 2 (over y), gy: 4 (over z), gz: 4 (over x, core).
Axes of the slice: x: 2, y: 2, z: 4, core: 2. Of those that a mesh axis runs over, the one named last changes fastest.
Arguments:
- moments: float32 [32, 128, 16, 128], P('gx', ('gy', 'gz')), may hold values from -128 to 128, as said below
- stiffness: float32 [32, 128, 16], P('gx', ('gy', 'gz')), may hold values from 0.5 to 4
- damping: float32 [32, 128, 16], P('gx', ('gy', 'gz')), may hold values from 0.05 to 1
- density: float32 [32, 128, 16], P('gx', ('gy', 'gz')), may hold values from 0.5 to 1.5
- ritz_coeffs: float32 [128, 128], replicated, may hold values from -128 to 128
- shifts: float32 [128], replicated, may hold values from -1.5 to -0.3
Outputs:
- ritz_vectors: float32 [32, 128, 16, 128], P('gx', ('gy', 'gz'))
- ritz_residual: float32 [32, 128, 16, 128], P('gx', ('gy', 'gz'))
- stiff_proj: float32 [128, 128], replicated
- damp_proj: float32 [128, 128], replicated
- mass_proj: float32 [128, 128], replicated
- first_factor: float32 [128, 128], replicated
Inputs may be any that keep to these rules, and one draw needn't show every extreme that they name: `moments`: A real block of full column rank.
All inputs are finite; a program needn't handle non-finite values.
Results may differ from a plain program's by a relative error of at most 0.0004.
Values sent between devices are 32-bit elements; how exact they have to be, the bound alone decides.
A program may use at most 64 MiB of HBM per device.

v0:
```python
import jax
import jax.numpy as jnp
from jax import lax
from jax.sharding import PartitionSpec as P


def with_halo(cells, sides, width):
    for axis, dim in sides:
        count = lax.axis_size(axis)
        ends = count - 1
        head = lax.slice_in_dim(cells, 0, width, axis=dim)
        tail = lax.slice_in_dim(cells, cells.shape[dim] - width, cells.shape[dim], axis=dim)
        cells = jnp.concatenate(
            [
                lax.ppermute(tail, axis, [(i, (i + 1) % count) for i in range(ends)]),
                cells,
                lax.ppermute(head, axis, [((i + 1) % count, i) for i in range(ends)]),
            ],
            axis=dim,
        )
    return cells


def factorize(gram):
    count = gram.shape[0]
    index = jnp.arange(count, dtype=jnp.int32)

    def column_step(j, carry):
        work, lower = carry
        onehot = (index == j).astype(gram.dtype)
        column = jnp.sum(work * onehot[None, :], axis=1)
        pivot = jnp.sum(column * onehot)
        column = jnp.where(index >= j, column, jnp.zeros_like(column)) / jnp.sqrt(pivot)
        lower = lower + column[:, None] * onehot[None, :]
        work = work - column[:, None] * column[None, :]
        return (work, lower)

    start = (gram, jnp.zeros_like(gram))
    lower = lax.fori_loop(0, count, column_step, start)[1]

    def row_step(i, inverse):
        onehot = (index == i).astype(gram.dtype)
        row = jnp.sum(lower * onehot[:, None], axis=0)
        pivot = jnp.sum(row * onehot)
        rhs = onehot - jnp.sum(row[:, None] * inverse, axis=0)
        return inverse + onehot[:, None] * (rhs / pivot)[None, :]

    inverse = lax.fori_loop(0, count, row_step, jnp.zeros_like(gram))
    return (lower, inverse.T)


def matmul(left, right):
    return jnp.dot(left, right, precision=lax.Precision.HIGHEST)


def apply_stencils(flat, shape, stiff_col, dens_col):
    field = flat.reshape(shape)
    padded = with_halo(field, (("gx", 0), (("gy", "gz"), 1)), 1)
    near = padded[2:, 1:-1] + padded[:-2, 1:-1]
    near = near + padded[1:-1, 2:] + padded[1:-1, :-2]
    plane = jnp.zeros((shape[0], shape[1], 1, shape[3]), jnp.float32)
    near = near + jnp.concatenate([field[:, :, 1:], plane], axis=2)
    near = near + jnp.concatenate([plane, field[:, :, :-1]], axis=2)
    near = near.reshape(flat.shape)
    return ((6.0 + stiff_col) * flat - near, dens_col * flat + near / 12.0)


def local(moments, stiffness, damping, density, ritz_coeffs, shifts):
    shape = moments.shape
    cells = shape[0] * shape[1] * shape[2]
    width = shape[3]
    all_cells = cells * lax.axis_size("gx") * lax.axis_size("gy") * lax.axis_size("gz")
    flat = moments.reshape(cells, width)
    stiff_col = stiffness.reshape(cells, 1)
    damp_col = damping.reshape(cells, 1)
    dens_col = density.reshape(cells, 1)
    lower_one, first_inv = factorize(lax.psum(matmul(flat.T, flat), ("gx", "gy", "gz")))
    first_factor = lower_one.T / jnp.sqrt(jnp.float32(all_cells))
    basis_one = matmul(flat, first_inv)
    k_block, m_block = apply_stencils(basis_one, shape, stiff_col, dens_col)
    c_block = damp_col * basis_one
    gram_two, stiff_one, damp_one, mass_one = lax.psum(
        (
            matmul(basis_one.T, basis_one),
            matmul(basis_one.T, k_block),
            matmul(basis_one.T, c_block),
            matmul(basis_one.T, m_block),
        ),
        ("gx", "gy", "gz"),
    )
    second_inv = factorize(gram_two)[1]
    stiff_proj = matmul(second_inv.T, matmul(stiff_one, second_inv))
    damp_proj = matmul(second_inv.T, matmul(damp_one, second_inv))
    mass_proj = matmul(second_inv.T, matmul(mass_one, second_inv))
    coeffs = matmul(second_inv, ritz_coeffs)
    ritz = matmul(basis_one, coeffs)
    resid = matmul(k_block, coeffs)
    resid = resid + matmul(c_block, coeffs) * shifts
    resid = resid + matmul(m_block, coeffs) * (shifts * shifts)
    return (
        ritz.reshape(shape),
        resid.reshape(shape),
        stiff_proj,
        damp_proj,
        mass_proj,
        first_factor,
    )


def solution(mesh):
    return jax.shard_map(
        local,
        mesh=mesh,
        in_specs=(
            P("gx", ("gy", "gz"), None, None),
            P("gx", ("gy", "gz"), None),
            P("gx", ("gy", "gz"), None),
            P("gx", ("gy", "gz"), None),
            P(),
            P(),
        ),
        out_specs=(
            P("gx", ("gy", "gz"), None, None),
            P("gx", ("gy", "gz"), None, None),
            P(),
            P(),
            P(),
            P(),
        ),
        check_vma=False,
    )
```

profile of v0, /device:TPU:0, one launch (start us, length us, event | category | flops | bytes accessed | tf_op | source)
XLA Modules:
  0.0 1594.6 jit_solution(11436615384494239305)
XLA Ops:
  8.4 2.5 convolution_bitcast_fusion
  13.7 120.7 %all-reduce.6.cloned.1.call-done = f32[128,128]{1,0:T(8,128)} async-done(((f32[128,128]{1,0:T(8,128)}), f32[128,128]{1,0:T(8,128)}) %all-reduce.6.cloned.1.call-update) | async-done | bytes 65552 | tf_op jit(solution)/shard_map/psum | solution.py:77
  134.5 488.4 %while.64 = (s32[]{:T(128)}, f32[128,128]{1,0:T(8,128)}, f32[128,128]{1,0:T(8,128)S(1)}, s32[]{:T(128)}, s32[]{:T(128)}) while((s32[]{:T(128)}, f32[128,128]{1,0:T(8,128)}, f32[128,128]{1,0:T(8,128)S(1)}, s32[]{:T(128)}, s32[]{:T(128)}) %tuple.132), condition=%wide.region_4.5_spmd.clone.clone, body=%wide.region_1.4_spmd.clone.clone.sunk | while | flops 115586 | bytes 331875 | solution.py:39
  136.7 1.5 select_add_fusion.4
  144.4 1.5 select_add_fusion.4
  152.0 1.5 select_add_fusion.4
  159.6 1.5 select_add_fusion.4
  163.4 1.5 select_add_fusion.4
  171.1 1.5 select_add_fusion.4
  178.7 1.5 select_add_fusion.4
  186.3 1.5 select_add_fusion.4
  194.0 1.5 select_add_fusion.4
  201.6 1.5 select_add_fusion.4
  209.2 1.5 select_add_fusion.4
  216.9 1.5 select_add_fusion.4
  224.5 1.5 select_add_fusion.4
  622.9 202.8 %while.62 = (s32[]{:T(128)}, f32[128,128]{1,0:T(8,128)S(1)}, f32[128,128]{1,0:T(8,128)S(1)}, s32[]{:T(128)}, s32[]{:T(128)}) while((s32[]{:T(128)}, f32[128,128]{1,0:T(8,128)S(1)}, f32[128,128]{1,0:T(8,128)S(1)}, s32[]{:T(128)}, s32[]{:T(128)}) %tuple.135), condition=%wide.region_9.10_spmd.clone, body=%wide.region_5.9_spmd.clone.sunk | while | flops 131970 | bytes 267356 | solution.py:48
  829.8 4.5 collective-permute-start.1
  834.3 1.6 fusion.39
  835.9 1.7 fusion.21
  839.0 3.9 collective-permute-start.3
  842.9 1.6 fusion.42
  845.8 1.6 copy.18
  847.4 1.7 fusion.28
  849.1 1.7 fusion.26
  851.5 127.3 %all-reduce.8.cloned.1.call-done = (f32[128,128]{1,0:T(8,128)}, f32[128,128]{1,0:T(8,128)}, f32[128,128]{1,0:T(8,128)}, f32[128,128]{1,0:T(8,128)}) async-done(((f32[128,128]{1,0:T(8,128)}, f32[128,128]{1,0:T(8,128)}, f32[128,128]{1,0:T(8,128)}, f32[128,128]{1,0:T(8,128)}), (f32[128,128]{1,0:T(8,128)}, f32[128,128]{1,0:T(8,128)}, f32[128,128]{1,0:T(8,128)}, ...) | async-done | bytes 262160 | tf_op jit(solution)/shard_map/psum | solution.py:82
  978.8 393.4 %while.65 = (s32[]{:T(128)}, f32[128,128]{1,0:T(8,128)}, f32[128,128]{1,0:T(8,128)S(1)}, s32[]{:T(128)}, s32[]{:T(128)}) while((s32[]{:T(128)}, f32[128,128]{1,0:T(8,128)}, f32[128,128]{1,0:T(8,128)S(1)}, s32[]{:T(128)}, s32[]{:T(128)}) %tuple.138), condition=%wide.region_14.15_spmd.clone.clone, body=%wide.region_11.14_spmd.clone.clone.sunk | while | flops 115586 | bytes 856219 | solution.py:39
  1372.2 202.7 %while.63 = (s32[]{:T(128)}, f32[128,128]{1,0:T(8,128)S(1)}, f32[128,128]{1,0:T(8,128)S(1)}, s32[]{:T(128)}, s32[]{:T(128)}) while((s32[]{:T(128)}, f32[128,128]{1,0:T(8,128)S(1)}, f32[128,128]{1,0:T(8,128)S(1)}, s32[]{:T(128)}, s32[]{:T(128)}) %tuple.141), condition=%wide.region_19.0_spmd.clone, body=%wide.region_15.19_spmd.clone.sunk | while | flops 131970 | bytes 267356 | solution.py:48
  1575.2 1.8 fusion.27
  1577.0 2.8 fusion.44
  1583.2 1.8 fusion.15
  1585.0 2.8 fusion.14
  (3378 shorter events, 1085.3 us)
Async XLA Ops:
  7.2 127.3 %all-reduce.6.cloned.1.call-start = ((), (), s32[]{:S(2)}) async-start(), calls=%async_computation | async-start | bytes 131072 | tf_op jit(solution)/shard_map/psum | solution.py:77
  10.9 967.9 %all-reduce.8.cloned.1.call-start = ((), (), s32[]{:S(2)}) async-start(), calls=%async_computation.1 | async-start | bytes 524288 | tf_op jit(solution)/shard_map/psum | solution.py:82
  827.8 9.9 collective-permute-start
  829.8 7.9 collective-permute-start.1
  837.7 6.8 collective-permute-start.2
  839.0 5.5 copy-start.3
  839.0 5.5 copy-start.4
  839.0 5.5 collective-permute-start.3
  984.9 2.3 copy-start.1
  988.0 2.3 copy-start.1
  991.1 2.3 copy-start.1
  1000.3 2.3 copy-start.1
  1003.4 2.3 copy-start.1
  1006.4 2.3 copy-start.1
  1015.7 2.3 copy-start.1
  1018.7 2.3 copy-start.1
  1021.8 2.3 copy-start.1
  1031.0 2.3 copy-start.1
  1034.1 2.3 copy-start.1
  1043.3 2.3 copy-start.1
  1046.4 2.3 copy-start.1
  1049.5 2.3 copy-start.1
  1058.7 2.3 copy-start.1
  1061.8 2.3 copy-start.1
  1064.8 2.3 copy-start.1
  1074.1 2.3 copy-start.1
  1077.1 2.3 copy-start.1
  1080.2 2.3 copy-start.1
  1089.4 2.3 copy-start.1
  1092.5 2.3 copy-start.1
  1372.2 202.7 %copy-start.6 = (f32[128,128]{1,0:T(8,128)S(1)}, f32[128,128]{1,0:T(8,128)}, u32[]{:S(2)}) copy-start(f32[128,128]{1,0:T(8,128)} %param.18) | copy-start | bytes 196612
  1577.0 2.8 copy-start.9
  (244 other events, 338.7 us)
Sparse Core Ops, SparseCore 0:
  14.2 120.2 all-reduce.5
  850.9 127.7 all-reduce.7
where the time goes:
time: 1620 us; the launch traced here: 1590 us
  other arithmetic  1010 us (62%)
  waiting for transfers between devices  248 us (15%)
  loops' own time  197 us (12%)
  local copies, waits for them, and re-layouts  87.3 us (5%)
  matrix products  22.9 us (1%)
    reduce_sum x256, other arithmetic, column_step(): column = jnp.sum(work * onehot[None, :], axis=1)  249 us
    add x256, other arithmetic, column_step(): lower = lower + column[:, None] * onehot[None, :]  209 us
    another operation x2, loops' own time, factorize(): lower = lax.fori_loop(0, count, column_step, start)[1]  186 us
    div x256, other arithmetic, row_step(): return inverse + onehot[:, None] * (rhs / pivot)[None, :]  166 us
    reduce_sum x256, other arithmetic, column_step(): pivot = jnp.sum(column * onehot)  157 us
    reduce_sum x256, other arithmetic, row_step(): pivot = jnp.sum(row * onehot)  155 us
    psum x1, waiting for transfers between devices, local(): lax.psum((matmul(basis_one.T, basis_one), matmul(basis_one.T, k_block), m...  127 us
    psum x1, waiting for transfers between devices, local(): lax.psum(matmul(flat.T, flat), ('gx', 'gy', 'gz'))  121 us
  transfers between devices with their start and end apart: 6, of which 2 were waited for; matrix products, arithmetic and copies ran while one was open for 0% of the time, Pallas kernels for 0%

commit v1 on v0

--- a/solution.py
+++ b/solution.py
@@ -80,13 +80,16 @@
     k_block, m_block = apply_stencils(basis_one, shape, stiff_col, dens_col)
     c_block = damp_col * basis_one
     gram_two, stiff_one, damp_one, mass_one = lax.psum(
-        (
-            matmul(basis_one.T, basis_one),
-            matmul(basis_one.T, k_block),
-            matmul(basis_one.T, c_block),
-            matmul(basis_one.T, m_block),
+        lax.psum(
+            (
+                matmul(basis_one.T, basis_one),
+                matmul(basis_one.T, k_block),
+                matmul(basis_one.T, c_block),
+                matmul(basis_one.T, m_block),
+            ),
+            ("gy", "gz"),
         ),
-        ("gx", "gy", "gz"),
+        "gx",
     )
     second_inv = factorize(gram_two)[1]
     stiff_proj = matmul(second_inv.T, matmul(stiff_one, second_inv))

time: 1620 us -> 1510 us (0.932)
  other arithmetic: 1010 us -> 836 us
  local copies, waits for them, and re-layouts: 87.3 us -> 164 us
    add x256, other arithmetic: 209 us -> 23.2 us  [column_step(): lower = lower + column[:, None] * onehot[None, :]]
    while x512 -> x1024, local copies, waits for them, and re-layouts: 78.8 us -> 158 us
    psum x1, waiting for transfers between devices: 127 us -> 93 us  [local(): lax.psum((matmul(basis_one.T, basis_one), matmul(basis_one.T, k_block), m...]
    psum x0 -> x1, waiting for transfers between devices: none -> 25.1 us  [local(): lax.psum(lax.psum((matmul(basis_one.T, basis_one), matmul(basis_one.T, k_...]
  transfers between devices with their start and end apart: 6 -> 7, of which waited for: 2 -> 4; matrix products, arithmetic and copies ran while one was open for 0% -> 0% of each run, Pallas kernels for 0% -> 0%
where the time goes in v1:
time: 1510 us; the launch traced here: 1490 us
  other arithmetic  836 us (55%)
  waiting for transfers between devices  240 us (16%)
  loops' own time  201 us (13%)
  local copies, waits for them, and re-layouts  164 us (11%)
  matrix products  22.9 us (2%)
    reduce_sum x256, other arithmetic, column_step(): column = jnp.sum(work * onehot[None, :], axis=1)  258 us
    another operation x2, loops' own time, factorize(): lower = lax.fori_loop(0, count, column_step, start)[1]  189 us
    div x256, other arithmetic, row_step(): return inverse + onehot[:, None] * (rhs / pivot)[None, :]  166 us
    while x1024, local copies, waits for them, and re-layouts  158 us
    reduce_sum x256, other arithmetic, column_step(): pivot = jnp.sum(column * onehot)  157 us
    reduce_sum x256, other arithmetic, row_step(): pivot = jnp.sum(row * onehot)  155 us
    psum x1, waiting for transfers between devices, local(): lax.psum(matmul(flat.T, flat), ('gx', 'gy', 'gz'))  122 us
    psum x1, waiting for transfers between devices, local(): lax.psum((matmul(basis_one.T, basis_one), matmul(basis_one.T, k_block), m...  93 us
  transfers between devices with their start and end apart: 7, of which 4 were waited for; matrix products, arithmetic and copies ran while one was open for 0% of the time, Pallas kernels for 0%

profile of v1, /device:TPU:0, one launch (start us, length us, event | category | flops | bytes accessed | tf_op | source)
XLA Modules:
  0.0 1488.5 jit_solution(18198185822533773569)
XLA Ops:
  7.2 1.2 copy-done
  8.4 2.5 convolution_bitcast_fusion
  12.7 121.8 %all-reduce.8.cloned.1.call-done = f32[128,128]{1,0:T(8,128)} async-done(((f32[128,128]{1,0:T(8,128)}), f32[128,128]{1,0:T(8,128)}) %all-reduce.8.cloned.1.call-update) | async-done | bytes 65552 | tf_op jit(solution)/shard_map/psum | solution.py:77
  134.5 392.6 %while.64 = (s32[]{:T(128)}, f32[128,128]{1,0:T(8,128)}, f32[128,128]{1,0:T(8,128)S(1)}, s32[]{:T(128)}, s32[]{:T(128)}) while((s32[]{:T(128)}, f32[128,128]{1,0:T(8,128)}, f32[128,128]{1,0:T(8,128)S(1)}, s32[]{:T(128)}, s32[]{:T(128)}) %tuple.132), condition=%wide.region_4.5_spmd.clone.clone, body=%wide.region_1.4_spmd.clone.clone.sunk | while | flops 115586 | bytes 856219 | solution.py:39
  527.1 202.8 %while.62 = (s32[]{:T(128)}, f32[128,128]{1,0:T(8,128)S(1)}, f32[128,128]{1,0:T(8,128)S(1)}, s32[]{:T(128)}, s32[]{:T(128)}) while((s32[]{:T(128)}, f32[128,128]{1,0:T(8,128)S(1)}, f32[128,128]{1,0:T(8,128)S(1)}, s32[]{:T(128)}, s32[]{:T(128)}) %tuple.135), condition=%wide.region_9.10_spmd.clone, body=%wide.region_5.9_spmd.clone.sunk | while | flops 131970 | bytes 267356 | solution.py:48
  729.8 1.0 fusion.41
  731.3 1.3 collective-permute-start
  732.7 4.5 collective-permute-start.1
  737.5 1.7 fusion.21
  739.5 1.3 collective-permute-start.2
  740.8 3.3 collective-permute-start.3
  744.1 1.6 fusion.42
  745.7 1.3 fusion.18
  747.0 1.6 copy.18
  748.6 1.7 fusion.28
  750.3 1.7 fusion.26
  752.2 93.0 %all-reduce.10.cloned.1.call-done = (f32[128,128]{1,0:T(8,128)}, f32[128,128]{1,0:T(8,128)}, f32[128,128]{1,0:T(8,128)}, f32[128,128]{1,0:T(8,128)}) async-done(((f32[128,128]{1,0:T(8,128)}, f32[128,128]{1,0:T(8,128)}, f32[128,128]{1,0:T(8,128)}, f32[128,128]{1,0:T(8,128)}), (f32[128,128]{1,0:T(8,128)}, f32[128,128]{1,0:T(8,128)}, f32[128,128]{1,0:T(8,128)}, ...) | async-done | bytes 262160 | tf_op jit(solution)/shard_map/psum | solution.py:83
  846.6 25.1 %all-reduce.12.cloned.1.call-done = (f32[128,128]{1,0:T(8,128)}, f32[128,128]{1,0:T(8,128)}, f32[128,128]{1,0:T(8,128)}, f32[128,128]{1,0:T(8,128)}) async-done(((f32[128,128]{1,0:T(8,128)}, f32[128,128]{1,0:T(8,128)}, f32[128,128]{1,0:T(8,128)}, f32[128,128]{1,0:T(8,128)}), (f32[128,128]{1,0:T(8,128)}, f32[128,128]{1,0:T(8,128)}, f32[128,128]{1,0:T(8,128)}, ...) | async-done | bytes 262160 | tf_op jit(solution)/shard_map/psum | solution.py:82
  871.7 394.6 %while.65 = (s32[]{:T(128)}, f32[128,128]{1,0:T(8,128)}, f32[128,128]{1,0:T(8,128)S(1)}, s32[]{:T(128)}, s32[]{:T(128)}) while((s32[]{:T(128)}, f32[128,128]{1,0:T(8,128)}, f32[128,128]{1,0:T(8,128)S(1)}, s32[]{:T(128)}, s32[]{:T(128)}) %tuple.138), condition=%wide.region_15.16_spmd.clone.clone, body=%wide.region_12.15_spmd.clone.clone.sunk | while | flops 115586 | bytes 856219 | solution.py:39
  874.8 1.0 multiply_reduce_fusion.17
  881.0 1.0 multiply_reduce_fusion.17
  887.2 1.0 multiply_reduce_fusion.17
  896.4 1.0 multiply_reduce_fusion.17
  902.6 1.0 multiply_reduce_fusion.17
  911.8 1.0 multiply_reduce_fusion.17
  918.0 1.0 multiply_reduce_fusion.17
  924.2 1.0 multiply_reduce_fusion.17
  1266.3 202.8 %while.63 = (s32[]{:T(128)}, f32[128,128]{1,0:T(8,128)S(1)}, f32[128,128]{1,0:T(8,128)S(1)}, s32[]{:T(128)}, s32[]{:T(128)}) while((s32[]{:T(128)}, f32[128,128]{1,0:T(8,128)S(1)}, f32[128,128]{1,0:T(8,128)S(1)}, s32[]{:T(128)}, s32[]{:T(128)}) %tuple.141), condition=%wide.region_20.0_spmd.clone, body=%wide.region_16.20_spmd.clone.sunk | while | flops 131970 | bytes 267356 | solution.py:48
  1469.4 1.8 fusion.27
  1471.2 2.8 fusion.44
  1477.3 1.8 fusion.15
  1479.1 2.8 fusion.14
  (3883 shorter events, 992.2 us)
Async XLA Ops:
  7.2 127.3 %all-reduce.8.cloned.1.call-start = ((), (), s32[]{:S(2)}) async-start(), calls=%async_computation | async-start | bytes 131072 | tf_op jit(solution)/shard_map/psum | solution.py:77
  10.9 834.3 %all-reduce.10.cloned.1.call-start = ((), (), s32[]{:S(2)}) async-start(), calls=%async_computation.1 | async-start | bytes 524288 | tf_op jit(solution)/shard_map/psum | solution.py:83
  731.3 7.9 collective-permute-start
  732.7 6.8 collective-permute-start.1
  739.5 6.2 collective-permute-start.2
  740.8 4.9 collective-permute-start.3
  752.0 119.8 %all-reduce.12.cloned.1.call-start = ((), (), s32[]{:S(2)}) async-start(), calls=%async_computation.2 | async-start | bytes 524288 | tf_op jit(solution)/shard_map/psum | solution.py:82
  871.7 2.3 copy-start.1
  874.8 2.3 copy-start.1
  877.9 2.3 copy-start.1
  881.0 2.3 copy-start.1
  884.1 2.3 copy-start.1
  887.2 2.3 copy-start.1
  893.3 2.3 copy-start.1
  896.4 2.3 copy-start.1
  899.5 2.3 copy-start.1
  902.6 2.3 copy-start.1
  905.7 2.3 copy-start.1
  908.7 2.3 copy-start.1
  911.8 2.3 copy-start.1
  914.9 2.3 copy-start.1
  918.0 2.3 copy-start.1
  921.1 2.3 copy-start.1
  924.2 2.3 copy-start.1
  930.3 2.3 copy-start.1
  933.4 2.3 copy-start.1
  936.5 2.3 copy-start.1
  939.6 2.3 copy-start.1
  942.6 2.3 copy-start.1
  945.7 2.3 copy-start.1
  1266.3 202.8 %copy-start.5 = (f32[128,128]{1,0:T(8,128)S(1)}, f32[128,128]{1,0:T(8,128)}, u32[]{:S(2)}) copy-start(f32[128,128]{1,0:T(8,128)} %param.18) | copy-start | bytes 196612
  1471.2 2.8 copy-start.8
  (496 other events, 712.0 us)
Sparse Core Ops, SparseCore 0:
  14.2 120.2 all-reduce.7
  752.1 93.0 all-reduce.9
  847.6 24.0 all-reduce.11

commit v2 on v0

--- a/solution.py
+++ b/solution.py
@@ -74,7 +74,9 @@
     stiff_col = stiffness.reshape(cells, 1)
     damp_col = damping.reshape(cells, 1)
     dens_col = density.reshape(cells, 1)
-    lower_one, first_inv = factorize(lax.psum(matmul(flat.T, flat), ("gx", "gy", "gz")))
+    lower_one, first_inv = factorize(
+        jnp.sum(lax.all_gather(matmul(flat.T, flat), ("gx", "gy", "gz")), axis=0)
+    )
     first_factor = lower_one.T / jnp.sqrt(jnp.float32(all_cells))
     basis_one = matmul(flat, first_inv)
     k_block, m_block = apply_stencils(basis_one, shape, stiff_col, dens_col)

time: 1620 us -> 1350 us (0.83)
  other arithmetic: 1010 us -> 901 us
  local copies, waits for them, and re-layouts: 87.3 us -> 7.04 us
  waiting for transfers between devices: 248 us -> 185 us
    psum x1 -> x0, waiting for transfers between devices: 121 us -> none  [local(): lax.psum(matmul(flat.T, flat), ('gx', 'gy', 'gz'))]
    reduce_sum x256, other arithmetic: 249 us -> 134 us  [column_step(): column = jnp.sum(work * onehot[None, :], axis=1)]
    while x512 -> x0, local copies, waits for them, and re-layouts: 78.8 us -> none
    all_gather x0 -> x1, waiting for transfers between devices: none -> 58.3 us  [local(): lax.all_gather(matmul(flat.T, flat), ('gx', 'gy', 'gz'))]
  transfers between devices with their start and end apart: 6 -> 6, of which waited for: 2 -> 2; matrix products, arithmetic and copies ran while one was open for 0% -> 1% of each run, Pallas kernels for 0% -> 0%
where the time goes in v2:
time: 1350 us; the launch traced here: 1340 us
  other arithmetic  901 us (67%)
  loops' own time  197 us (15%)
  waiting for transfers between devices  185 us (14%)
  matrix products  22.9 us (2%)
  between operations  14.4 us (1%)
    add x256, other arithmetic, column_step(): lower = lower + column[:, None] * onehot[None, :]  210 us
    another operation x2, loops' own time, factorize(): lower = lax.fori_loop(0, count, column_step, start)[1]  186 us
    div x256, other arithmetic, row_step(): return inverse + onehot[:, None] * (rhs / pivot)[None, :]  166 us
    reduce_sum x256, other arithmetic, column_step(): pivot = jnp.sum(column * onehot)  157 us
    reduce_sum x256, other arithmetic, row_step(): pivot = jnp.sum(row * onehot)  155 us
    reduce_sum x256, other arithmetic, column_step(): column = jnp.sum(work * onehot[None, :], axis=1)  134 us
    psum x1, waiting for transfers between devices, local(): lax.psum((matmul(basis_one.T, basis_one), matmul(basis_one.T, k_block), m...  127 us
    all_gather x1, waiting for transfers between devices, local(): lax.all_gather(matmul(flat.T, flat), ('gx', 'gy', 'gz'))  58.3 us
  transfers between devices with their start and end apart: 6, of which 2 were waited for; matrix products, arithmetic and copies ran while one was open for 1% of the time, Pallas kernels for 0%

profile of v2, /device:TPU:0, one launch (start us, length us, event | category | flops | bytes accessed | tf_op | source)
XLA Modules:
  0.0 1338.2 jit_solution(5366377119246734215)
XLA Ops:
  8.4 2.5 convolution_bitcast_fusion
  12.4 58.3 %all-gather.3.cloned.1.call-done = f32[4096,128]{1,0:T(8,128)} async-done(((f32[128,128]{1,0:T(8,128)}), f32[4096,128]{1,0:T(8,128)}) %all-gather.3.cloned.1.call-update) | async-done | bytes 2097168 | tf_op jit(solution)/shard_map/all_gather | solution.py:78
  70.7 1.7 reduce_sum.139
  72.4 199.3 %while.64 = (s32[]{:T(128)}, f32[128,128]{1,0:T(8,128)S(1)}, f32[128,128]{1,0:T(8,128)S(1)}, s32[]{:T(128)}, s32[]{:T(128)}) while((s32[]{:T(128)}, f32[128,128]{1,0:T(8,128)S(1)}, f32[128,128]{1,0:T(8,128)S(1)}, s32[]{:T(128)}, s32[]{:T(128)}) %tuple.132), condition=%wide.region_4.5_spmd.clone.clone, body=%wide.region_1.4_spmd.clone.clone.sunk | while | flops 115586 | bytes 331875 | solution.py:39
  271.7 202.8 %while.62 = (s32[]{:T(128)}, f32[128,128]{1,0:T(8,128)S(1)}, f32[128,128]{1,0:T(8,128)S(1)}, s32[]{:T(128)}, s32[]{:T(128)}) while((s32[]{:T(128)}, f32[128,128]{1,0:T(8,128)S(1)}, f32[128,128]{1,0:T(8,128)S(1)}, s32[]{:T(128)}, s32[]{:T(128)}) %tuple.135), condition=%wide.region_9.10_spmd.clone, body=%wide.region_5.9_spmd.clone.sunk | while | flops 131970 | bytes 267356 | solution.py:48
  478.6 4.5 collective-permute-start.1
  483.1 1.6 fusion.39
  484.7 1.7 fusion.21
  487.9 3.2 collective-permute-start.3
  491.2 1.6 fusion.42
  494.1 1.6 copy.18
  495.6 1.7 fusion.28
  497.4 1.7 fusion.26
  499.7 126.9 %all-reduce.5.cloned.1.call-done = (f32[128,128]{1,0:T(8,128)}, f32[128,128]{1,0:T(8,128)}, f32[128,128]{1,0:T(8,128)}, f32[128,128]{1,0:T(8,128)}) async-done(((f32[128,128]{1,0:T(8,128)}, f32[128,128]{1,0:T(8,128)}, f32[128,128]{1,0:T(8,128)}, f32[128,128]{1,0:T(8,128)}), (f32[128,128]{1,0:T(8,128)}, f32[128,128]{1,0:T(8,128)}, f32[128,128]{1,0:T(8,128)}, ...) | async-done | bytes 262160 | tf_op jit(solution)/shard_map/psum | solution.py:84
  626.6 489.2 %while.65 = (s32[]{:T(128)}, f32[128,128]{1,0:T(8,128)}, f32[128,128]{1,0:T(8,128)S(1)}, s32[]{:T(128)}, s32[]{:T(128)}) while((s32[]{:T(128)}, f32[128,128]{1,0:T(8,128)}, f32[128,128]{1,0:T(8,128)S(1)}, s32[]{:T(128)}, s32[]{:T(128)}) %tuple.138), condition=%wide.region_14.15_spmd.clone.clone, body=%wide.region_11.14_spmd.clone.clone.sunk | while | flops 115586 | bytes 331875 | solution.py:39
  628.9 1.6 select_add_fusion.5
  644.2 1.6 select_add_fusion.5
  655.6 1.6 select_add_fusion.5
  659.4 1.6 select_add_fusion.5
  670.9 1.6 select_add_fusion.5
  686.2 1.6 select_add_fusion.5
  701.5 1.6 select_add_fusion.5
  716.8 1.6 select_add_fusion.5
  728.2 1.6 select_add_fusion.5
  732.1 1.6 select_add_fusion.5
  743.5 1.6 select_add_fusion.5
  758.8 1.6 select_add_fusion.5
  1115.8 202.7 %while.63 = (s32[]{:T(128)}, f32[128,128]{1,0:T(8,128)S(1)}, f32[128,128]{1,0:T(8,128)S(1)}, s32[]{:T(128)}, s32[]{:T(128)}) while((s32[]{:T(128)}, f32[128,128]{1,0:T(8,128)S(1)}, f32[128,128]{1,0:T(8,128)S(1)}, s32[]{:T(128)}, s32[]{:T(128)}) %tuple.141), condition=%wide.region_19.0_spmd.clone, body=%wide.region_15.19_spmd.clone.sunk | while | flops 131970 | bytes 267356 | solution.py:48
  1318.9 1.8 fusion.27
  1320.7 2.8 fusion.44
  1326.8 1.8 fusion.15
  1328.6 2.8 fusion.14
  (2867 shorter events, 892.0 us)
Async XLA Ops:
  7.2 1.2 copy-start
  7.2 3.8 copy-start.8
  7.2 3.9 copy-start.10
  7.2 4.6 copy-start.9
  7.2 4.6 copy-start.12
  7.2 63.4 %all-gather.3.cloned.1.call-start = ((), (), s32[]{:S(2)}) async-start(), calls=%async_computation | async-start | bytes 2162688 | tf_op jit(solution)/shard_map/all_gather | solution.py:78
  10.9 615.7 %all-reduce.5.cloned.1.call-start = ((), (), s32[]{:S(2)}) async-start(), calls=%async_computation.1 | async-start | bytes 524288 | tf_op jit(solution)/shard_map/psum | solution.py:84
  476.6 9.9 collective-permute-start
  478.6 7.9 collective-permute-start.1
  486.4 6.4 copy-start.1
  486.4 6.4 copy-start.2
  486.5 6.3 collective-permute-start.2
  487.9 4.9 collective-permute-start.3
  495.6 1.7 copy-start.3
  499.1 819.5 %copy-start.4 = (f32[128,128]{1,0:T(8,128)S(1)}, f32[128,128]{1,0:T(8,128)}, u32[]{:S(2)}) copy-start(f32[128,128]{1,0:T(8,128)} %param.18) | copy-start | bytes 196612
  1318.8 4.6 copy-start.7
  1318.8 5.7 copy-start.6
  1320.7 5.0 copy-start.5
  1320.7 6.1 copy-start.13
  1323.7 4.9 copy-start.11
Sparse Core Ops, SparseCore 0:
  11.5 59.1 all-gather.2
  499.2 127.3 all-reduce.4
